TPU v7x, 32 devices: a whole 2x2x4 slice. The times are simulated.
32 devices in a mesh: gx: 8 (over z, y), gy: 4 (over x, core).
Axes of the slice: x: 2, y: 2, z: 4, core: 2. Of those that a mesh axis runs over, the one named last changes fastest.
Arguments:
- cell_state: float32 [39, 65536], P(None, ('gx', 'gy')), may hold values from 0.1 to 2
- coupling: float32 [39, 39], replicated, may hold values from -1 to 1
- basal_rate: float32 [39], replicated, may hold values from 0.1 to 1
- half_sat: float32 [39], replicated, may hold values from 0.2 to 2
- decay_rate: float32 [39], replicated, may hold values from 0.1 to 1
- uptake_weight: float32 [39], replicated, may hold values from -1 to 1
- agent_counts: int32 [32], P(('gx', 'gy')), may hold values from 512 to 2048, as said below
- divider_ids: int32 [4096], P(('gx', 'gy')), may hold values from 0 to 2047, as said below
- destinations: int32 [4096, 1], P(('gx', 'gy')), may hold values from 0 to 7; in each aligned block of 128 rows (0 to 127, 128 to 255, ...) at most 32 rows name the same one
- voxel_index: int32 [65536], P(('gx', 'gy')), may hold values from 0 to 196607, as said below
- oxygen: float32 [64, 64, 512], P(None, 'gx', 'gy'), may hold values from 0.5 to 1.5
Outputs:
- new_state: float32 [39, 65536], P(None, ('gx', 'gy'))
- daughter_state: float32 [39, 8192], P(None, ('gx', 'gy'))
- new_oxygen: float32 [64, 64, 512], P(None, 'gx', 'gy')
Inputs may be any that keep to these rules, and one draw needn't show every extreme that they name: Live agents of a device are its first agent_counts slots; at least 512, and some device holds 2048. `divider_ids`: each entry is below the live count of its device; entries may repeat. `destinations`: within the list of one device no x-slab is named by more than 32 rows. `voxel_index`: the named voxel lies in the agent's own x-slab or an adjacent one (s = 0, 1 or 2) and inside the grid, with y inside its device's range.
All inputs are finite; a program needn't handle non-finite values.
Results may differ from a plain program's by a relative error of at most 0.0011.
Values may be sent and summed in bfloat16 or wider, within the bound.
No kernel may reach another device: no remote copies, remote signals or barrier semaphores. Data moves between devices by JAX's collectives and lax.ppermute only.
A program may use at most 64 MiB of HBM per device.

v0:
```python
import math
import jax
import jax.numpy as jnp
from jax import lax
from jax.sharding import PartitionSpec as P

time_step = 0.25
diffusion_number = 0.16


def shifted(block, axis, distance):
    devices = range(lax.axis_size(axis))
    route = [(i - distance, i) for i in devices if i - distance in devices]
    return lax.ppermute(block, axis, route)


def with_halo(cells, sides, width):
    for axis, dim in sides:
        count = lax.axis_size(axis)
        ends = count - 1
        head = lax.slice_in_dim(cells, 0, width, axis=dim)
        tail = lax.slice_in_dim(cells, cells.shape[dim] - width, cells.shape[dim], axis=dim)
        cells = jnp.concatenate(
            [
                lax.ppermute(tail, axis, [(i, (i + 1) % count) for i in range(ends)]),
                cells,
                lax.ppermute(head, axis, [((i + 1) % count, i) for i in range(ends)]),
            ],
            axis=dim,
        )
    return cells


def network_rates(current, coupling, basal_rate, half_sat, decay_rate):
    square = current * current
    occupancy = square / (half_sat[:, None] * half_sat[:, None] + square)
    drive_sum = jnp.dot(
        coupling, occupancy, precision=lax.Precision.HIGHEST, preferred_element_type=jnp.float32
    )
    return basal_rate[:, None] + drive_sum - decay_rate[:, None] * current


def advance(current, coupling, basal_rate, half_sat, decay_rate):
    for substep in range(2):
        middle = current + 0.5 * time_step * network_rates(
            current, coupling, basal_rate, half_sat, decay_rate
        )
        current = current + time_step * network_rates(
            middle, coupling, basal_rate, half_sat, decay_rate
        )
    return current


def deposit_rows(weights, row_index, columns, row_count, column_count):
    block_size = math.gcd(weights.shape[0], 512)
    block_count = weights.shape[0] // block_size
    row_ids = jnp.arange(row_count, dtype=jnp.int32)
    column_ids = jnp.arange(column_count, dtype=jnp.int32)

    def one_block(running, block_turn):
        start = block_turn * block_size
        piece_weight = lax.dynamic_slice_in_dim(weights, start, block_size)
        piece_row = lax.dynamic_slice_in_dim(row_index, start, block_size)
        piece_column = lax.dynamic_slice_in_dim(columns, start, block_size)
        left_table = (piece_row[:, None] == row_ids[None, :]).astype(jnp.bfloat16)
        right_table = (piece_column[:, None] == column_ids[None, :]).astype(
            jnp.bfloat16
        ) * piece_weight[:, None]
        product = lax.dot_general(
            left_table, right_table, (((0,), (0,)), ((), ())), preferred_element_type=jnp.float32
        )
        return (running + product, None)

    running, unused = lax.scan(
        one_block, jnp.zeros((row_count, column_count), jnp.float32), jnp.arange(block_count)
    )
    return running


def sweep_once(padded):
    z_padded = jnp.pad(padded, ((1, 1), (0, 0), (0, 0)))
    center = padded[:, 1:-1, 1:-1]
    beside = z_padded[2:, 1:-1, 1:-1] + z_padded[:-2, 1:-1, 1:-1]
    beside = beside + padded[:, 2:, 1:-1] + padded[:, :-2, 1:-1]
    beside = beside + padded[:, 1:-1, 2:] + padded[:, 1:-1, :-2]
    return center + diffusion_number * (beside - 6.0 * center)


def shards(
    cell_state,
    coupling,
    basal_rate,
    half_sat,
    decay_rate,
    uptake_weight,
    agent_counts,
    divider_ids,
    destinations,
    voxel_index,
    oxygen,
):
    grid_count = lax.axis_size("gx")
    picks_count = divider_ids.shape[0]
    capacity = max(2, 2 * picks_count // grid_count)
    target_slab = destinations[:, 0]
    onehot = (target_slab[:, None] == jnp.arange(grid_count, dtype=jnp.int32)[None, :]).astype(
        jnp.int32
    )
    earlier = jnp.cumsum(onehot, axis=0) - onehot
    slot_rank = jnp.sum(earlier * onehot, axis=1)
    position = target_slab * capacity + slot_rank
    placing = (
        position[:, None] == jnp.arange(grid_count * capacity, dtype=jnp.int32)[None, :]
    ).astype(jnp.float32)
    mothers = jnp.take(cell_state, divider_ids, axis=1)
    outgoing = jnp.dot(
        mothers, placing, precision=lax.Precision.HIGHEST, preferred_element_type=jnp.float32
    )
    occupied = jnp.sum(placing, axis=0)[None, :]
    received, arrived = (
        lax.all_to_all(outgoing, "gx", split_axis=1, concat_axis=1, tiled=True),
        lax.all_to_all(occupied, "gx", split_axis=1, concat_axis=1, tiled=True),
    )
    new_state = advance(cell_state, coupling, basal_rate, half_sat, decay_rate)
    daughter_state = advance(received, coupling, basal_rate, half_sat, decay_rate) * arrived
    agents = cell_state.shape[1]
    drive_sum = jnp.dot(
        uptake_weight,
        new_state,
        precision=lax.Precision.HIGHEST,
        preferred_element_type=jnp.float32,
    )
    alive_mask = jnp.arange(agents, dtype=jnp.int32) < agent_counts[0]
    uptake = jnp.where(alive_mask, jax.nn.softplus(drive_sum), 0.0).astype(jnp.bfloat16)
    depth_cells, width_x, width_y = oxygen.shape
    slab_rows = depth_cells * width_x
    row_index = voxel_index // width_y
    columns = voxel_index % width_y
    partial_value = deposit_rows(uptake, row_index, columns, 3 * slab_rows, width_y).reshape(
        3, depth_cells, width_x, width_y
    )
    from_lower = shifted(partial_value[2].astype(jnp.bfloat16), "gx", 1).astype(jnp.float32)
    from_upper = shifted(partial_value[0].astype(jnp.bfloat16), "gx", -1).astype(jnp.float32)
    deposit = partial_value[1] + from_lower + from_upper
    oxygen_field = oxygen - deposit
    for sweep_turn in range(4):
        padded = with_halo(oxygen_field, (("gx", 1), ("gy", 2)), 1)
        oxygen_field = sweep_once(padded)
    return (new_state, daughter_state, oxygen_field)


def solution(mesh):
    return jax.shard_map(
        shards,
        mesh=mesh,
        in_specs=(
            P(None, ("gx", "gy")),
            P(),
            P(),
            P(),
            P(),
            P(),
            P(("gx", "gy")),
            P(("gx", "gy")),
            P(("gx", "gy"), None),
            P(("gx", "gy")),
            P(None, "gx", "gy"),
        ),
        out_specs=(P(None, ("gx", "gy")), P(None, ("gx", "gy")), P(None, "gx", "gy")),
        check_vma=False,
    )
```

profile of v0, /device:TPU:1, one launch (start us, length us, event | category | flops | bytes accessed | tf_op | source)
XLA Modules:
  0.0 136.2 jit_solution(7530949191528294205)
XLA Ops:
  6.1 12.0 %while.11 = (s32[]{:T(128)}, f32[1536,128]{1,0:T(8,128)S(1)}, s32[4]{0:T(128)S(1)}, s32[2048]{0:T(1024)S(1)}, s32[2048]{0:T(1024)S(1)}, /*index=5*/bf16[2048]{0:...) while((s32[]{:T(128)}, f32[1536,128]{1,0:T(8,128)S(1)}, s32[4]{0:T(128)S(1)}, ...), condition=%wide.region_4.5_spmd.clone, body=%wide.region_3.4_spmd.clone.sunk | while | flops 202637312 | bytes 1588405 | solution.py:74
  18.2 4.0 %collective-permute-start = (bf16[64,8,128]{2,1,0:T(8,128)(2,1)S(1)}, bf16[64,8,128]{2,1,0:T(8,128)(2,1)S(1)}, u32[]{:S(2)}, u32[]{:S(2)}) collective-permute-start(bf16[64,8,128]{2,1,0:T(8,128)(2,1)S(1)} %get-tuple-element.91), channel_id=1, source_target_pairs={{0,4},{4,8},{8,12},{12,16},{16,20},{20,24},{24,28},{1,5},{5,9},{9,... | collective-permute-start | bytes 393224 | tf_op jit(solution)/shard_map/ppermute | solution.py:14
  24.7 6.4 %all-to-all-start.1 = ((f32[1,8,32]{2,0,1:T(1,128)}), f32[1,8,32]{2,0,1:T(1,128)S(1)}, u32[]{:S(2)}, u32[]{:S(2)}) async-start(f32[1,8,32]{2,0,1:T(1,128)} %all_to_all.17), calls=%async_computation.1 | async-start | bytes 8192 | tf_op jit(solution)/shard_map/all_to_all | solution.py:122
  31.3 3.4 %collective-permute-start.2 = (f32[64,1,128]{2,1,0:T(1,128)S(1)}, f32[64,1,128]{2,1,0:T(1,128)S(1)}, u32[]{:S(2)}, u32[]{:S(2)}) collective-permute-start(f32[64,1,128]{2,1,0:T(1,128)S(1)} %get-tuple-element.99), channel_id=1, source_target_pairs={{0,4},{4,8},{8,12},{12,16},{16,20},{20,24},{24,28},{1,5},{5,9},{9,... | collective-permute-start | bytes 98312 | tf_op jit(solution)/shard_map/ppermute | solution.py:25
  36.0 3.3 %collective-permute-done.3 = f32[64,1,128]{2,1,0:T(1,128)S(1)} collective-permute-done((f32[64,1,128]{2,1,0:T(1,128)S(1)}, f32[64,1,128]{2,1,0:T(1,128)S(1)}, u32[]{:S(2)}, u32[]{:S(2)}) %collective-permute-start.3) | collective-permute-done | bytes 32800 | tf_op jit(solution)/shard_map/ppermute | solution.py:27
  40.5 6.2 %collective-permute-start.4 = (f32[64,10,1]{2,1,0:T(8,128)}, f32[64,10,1]{2,1,0:T(8,128)S(1)}, u32[]{:S(2)}, u32[]{:S(2)}) collective-permute-start(f32[64,10,1]{2,1,0:T(8,128)} %get-tuple-element.90), channel_id=1, source_target_pairs={{0,1},{1,2},{2,3},{4,5},{5,6},{6,7},{8,9},{9,10},{10,11},{12,13},{... | collective-permute-start | bytes 7688 | tf_op jit(solution)/shard_map/ppermute | solution.py:25
  46.7 1.9 %collective-permute-start.5 = (f32[64,10,1]{2,1,0:T(8,128)S(1)}, f32[64,10,1]{2,1,0:T(8,128)S(1)}, u32[]{:S(2)}, u32[]{:S(2)}) collective-permute-start(f32[64,10,1]{2,1,0:T(8,128)S(1)} %get-tuple-element.89), channel_id=1, source_target_pairs={{1,0},{2,1},{3,2},{5,4},{6,5},{7,6},{9,8},{10,9},{11,10},{13,12},{... | collective-permute-start | bytes 7688 | tf_op jit(solution)/shard_map/ppermute | solution.py:27
  49.7 3.5 %collective-permute-done.4 = f32[64,10,1]{2,1,0:T(8,128)S(1)} collective-permute-done((f32[64,10,1]{2,1,0:T(8,128)}, f32[64,10,1]{2,1,0:T(8,128)S(1)}, u32[]{:S(2)}, u32[]{:S(2)}) %collective-permute-start.4) | collective-permute-done | bytes 2592 | tf_op jit(solution)/shard_map/ppermute | solution.py:25
  53.1 4.1 %collective-permute-done.5 = f32[64,10,1]{2,1,0:T(8,128)S(1)} collective-permute-done((f32[64,10,1]{2,1,0:T(8,128)S(1)}, f32[64,10,1]{2,1,0:T(8,128)S(1)}, u32[]{:S(2)}, u32[]{:S(2)}) %collective-permute-start.5) | collective-permute-done | bytes 2592 | tf_op jit(solution)/shard_map/ppermute | solution.py:27
  59.3 4.0 %collective-permute-start.6 = (f32[64,1,128]{2,1,0:T(1,128)S(1)}, f32[64,1,128]{2,1,0:T(1,128)S(1)}, u32[]{:S(2)}, u32[]{:S(2)}) collective-permute-start(f32[64,1,128]{2,1,0:T(1,128)S(1)} %get-tuple-element.97), channel_id=1, source_target_pairs={{0,4},{4,8},{8,12},{12,16},{16,20},{20,24},{24,28},{1,5},{5,9},{9,... | collective-permute-start | bytes 98312 | tf_op jit(solution)/shard_map/ppermute | solution.py:25
  65.8 2.2 %collective-permute-done.7 = f32[64,1,128]{2,1,0:T(1,128)S(1)} collective-permute-done((f32[64,1,128]{2,1,0:T(1,128)S(1)}, f32[64,1,128]{2,1,0:T(1,128)S(1)}, u32[]{:S(2)}, u32[]{:S(2)}) %collective-permute-start.7) | collective-permute-done | bytes 32800 | tf_op jit(solution)/shard_map/ppermute | solution.py:27
  68.1 4.3 %all-to-all-start = ((f32[8,1,1248]{2,1,0:T(1,128)}), f32[8,1,1248]{2,1,0:T(1,128)S(1)}, u32[]{:S(2)}, u32[]{:S(2)}) async-start(f32[8,1,1248]{2,1,0:T(1,128)} %reshape.58), calls=%async_computation | async-start | bytes 81920 | tf_op jit(solution)/shard_map/all_to_all | solution.py:121
  72.6 3.5 %collective-permute-start.8 = (f32[64,10,1]{2,1,0:T(8,128)S(1)}, f32[64,10,1]{2,1,0:T(8,128)S(1)}, u32[]{:S(2)}, u32[]{:S(2)}) collective-permute-start(f32[64,10,1]{2,1,0:T(8,128)S(1)} %get-tuple-element.88), channel_id=1, source_target_pairs={{0,1},{1,2},{2,3},{4,5},{5,6},{6,7},{8,9},{9,10},{10,11},{12,13},{... | collective-permute-start | bytes 7688 | tf_op jit(solution)/shard_map/ppermute | solution.py:25
  82.2 4.4 %collective-permute-done.9 = f32[64,10,1]{2,1,0:T(8,128)S(1)} collective-permute-done((f32[64,10,1]{2,1,0:T(8,128)S(1)}, f32[64,10,1]{2,1,0:T(8,128)S(1)}, u32[]{:S(2)}, u32[]{:S(2)}) %collective-permute-start.9) | collective-permute-done | bytes 2592 | tf_op jit(solution)/shard_map/ppermute | solution.py:27
  88.0 3.7 %collective-permute-start.10 = (f32[64,1,128]{2,1,0:T(1,128)S(1)}, f32[64,1,128]{2,1,0:T(1,128)S(1)}, u32[]{:S(2)}, u32[]{:S(2)}) collective-permute-start(f32[64,1,128]{2,1,0:T(1,128)S(1)} %get-tuple-element.95), channel_id=1, source_target_pairs={{0,4},{4,8},{8,12},{12,16},{16,20},{20,24},{24,28},{1,5},{5,9},{9,... | collective-permute-start | bytes 98312 | tf_op jit(solution)/shard_map/ppermute | solution.py:25
  93.3 3.1 %collective-permute-done.11 = f32[64,1,128]{2,1,0:T(1,128)S(1)} collective-permute-done((f32[64,1,128]{2,1,0:T(1,128)S(1)}, f32[64,1,128]{2,1,0:T(1,128)S(1)}, u32[]{:S(2)}, u32[]{:S(2)}) %collective-permute-start.11) | collective-permute-done | bytes 32800 | tf_op jit(solution)/shard_map/ppermute | solution.py:27
  96.7 3.1 %collective-permute-start.12 = (f32[64,10,1]{2,1,0:T(8,128)S(1)}, f32[64,10,1]{2,1,0:T(8,128)S(1)}, u32[]{:S(2)}, u32[]{:S(2)}) collective-permute-start(f32[64,10,1]{2,1,0:T(8,128)S(1)} %get-tuple-element.86), channel_id=1, source_target_pairs={{0,1},{1,2},{2,3},{4,5},{5,6},{6,7},{8,9},{9,10},{10,11},{12,13},{... | collective-permute-start | bytes 7688 | tf_op jit(solution)/shard_map/ppermute | solution.py:25
  101.9 3.9 %collective-permute-done.12 = f32[64,10,1]{2,1,0:T(8,128)S(1)} collective-permute-done((f32[64,10,1]{2,1,0:T(8,128)S(1)}, f32[64,10,1]{2,1,0:T(8,128)S(1)}, u32[]{:S(2)}, u32[]{:S(2)}) %collective-permute-start.12) | collective-permute-done | bytes 2592 | tf_op jit(solution)/shard_map/ppermute | solution.py:25
  105.9 4.4 %collective-permute-done.13 = f32[64,10,1]{2,1,0:T(8,128)S(1)} collective-permute-done((f32[64,10,1]{2,1,0:T(8,128)S(1)}, f32[64,10,1]{2,1,0:T(8,128)S(1)}, u32[]{:S(2)}, u32[]{:S(2)}) %collective-permute-start.13) | collective-permute-done | bytes 2592 | tf_op jit(solution)/shard_map/ppermute | solution.py:27
  111.6 4.1 %collective-permute-start.14 = (f32[64,1,128]{2,1,0:T(1,128)S(1)}, f32[64,1,128]{2,1,0:T(1,128)S(1)}, u32[]{:S(2)}, u32[]{:S(2)}) collective-permute-start(f32[64,1,128]{2,1,0:T(1,128)S(1)} %get-tuple-element.93), channel_id=1, source_target_pairs={{0,4},{4,8},{8,12},{12,16},{16,20},{20,24},{24,28},{1,5},{5,9},{9,... | collective-permute-start | bytes 98312 | tf_op jit(solution)/shard_map/ppermute | solution.py:25
  117.3 3.1 %collective-permute-done.15 = f32[64,1,128]{2,1,0:T(1,128)S(1)} collective-permute-done((f32[64,1,128]{2,1,0:T(1,128)S(1)}, f32[64,1,128]{2,1,0:T(1,128)S(1)}, u32[]{:S(2)}, u32[]{:S(2)}) %collective-permute-start.15) | collective-permute-done | bytes 32800 | tf_op jit(solution)/shard_map/ppermute | solution.py:27
  120.6 3.1 %collective-permute-start.16 = (f32[64,10,1]{2,1,0:T(8,128)S(1)}, f32[64,10,1]{2,1,0:T(8,128)S(1)}, u32[]{:S(2)}, u32[]{:S(2)}) collective-permute-start(f32[64,10,1]{2,1,0:T(8,128)S(1)} %get-tuple-element.84), channel_id=1, source_target_pairs={{0,1},{1,2},{2,3},{4,5},{5,6},{6,7},{8,9},{9,10},{10,11},{12,13},{... | collective-permute-start | bytes 7688 | tf_op jit(solution)/shard_map/ppermute | solution.py:25
  126.5 3.3 %collective-permute-done.16 = f32[64,10,1]{2,1,0:T(8,128)S(1)} collective-permute-done((f32[64,10,1]{2,1,0:T(8,128)S(1)}, f32[64,10,1]{2,1,0:T(8,128)S(1)}, u32[]{:S(2)}, u32[]{:S(2)}) %collective-permute-start.16) | collective-permute-done | bytes 2592 | tf_op jit(solution)/shard_map/ppermute | solution.py:25
  129.8 4.4 %collective-permute-done.17 = f32[64,10,1]{2,1,0:T(8,128)S(1)} collective-permute-done((f32[64,10,1]{2,1,0:T(8,128)S(1)}, f32[64,10,1]{2,1,0:T(8,128)S(1)}, u32[]{:S(2)}, u32[]{:S(2)}) %collective-permute-start.17) | collective-permute-done | bytes 2592 | tf_op jit(solution)/shard_map/ppermute | solution.py:27
  (118 shorter events, 44.3 us)
Async XLA Ops:
  18.1 13.0 %copy-start.9 = (s32[128]{0:T(128)S(1)}, s32[128]{0:T(128)}, u32[]{:S(2)}) copy-start(s32[128]{0:T(128)} %param.20) | copy-start | bytes 1540
  18.1 13.1 %copy-start.5 = (f32[64,8,128]{2,1,0:T(8,128)S(1)}, f32[64,8,128]{2,1,0:T(8,128)}, u32[]{:S(2)}) copy-start(f32[64,8,128]{2,1,0:T(8,128)} %param.23) | copy-start | bytes 786436
  18.2 13.0 %collective-permute-start = (bf16[64,8,128]{2,1,0:T(8,128)(2,1)S(1)}, bf16[64,8,128]{2,1,0:T(8,128)(2,1)S(1)}, u32[]{:S(2)}, u32[]{:S(2)}) collective-permute-start(bf16[64,8,128]{2,1,0:T(8,128)(2,1)S(1)} %get-tuple-element.91), channel_id=1, source_target_pairs={{0,4},{4,8},{8,12},{12,16},{16,20},{20,24},{24,28},{1,5},{5,9},{9,... | collective-permute-start | bytes 393224 | tf_op jit(solution)/shard_map/ppermute | solution.py:14
  22.2 9.0 %collective-permute-start.1 = (bf16[64,8,128]{2,1,0:T(8,128)(2,1)S(1)}, bf16[64,8,128]{2,1,0:T(8,128)(2,1)S(1)}, u32[]{:S(2)}, u32[]{:S(2)}) collective-permute-start(bf16[64,8,128]{2,1,0:T(8,128)(2,1)S(1)} %get-tuple-element.92), channel_id=1, source_target_pairs={{4,0},{8,4},{12,8},{16,12},{20,16},{24,20},{28,24},{5,1},{9,5},{13... | collective-permute-start | bytes 393224 | tf_op jit(solution)/shard_map/ppermute | solution.py:14
  24.7 43.4 %all-to-all-start.1 = ((f32[1,8,32]{2,0,1:T(1,128)}), f32[1,8,32]{2,0,1:T(1,128)S(1)}, u32[]{:S(2)}, u32[]{:S(2)}) async-start(f32[1,8,32]{2,0,1:T(1,128)} %all_to_all.17), calls=%async_computation.1 | async-start | bytes 8192 | tf_op jit(solution)/shard_map/all_to_all | solution.py:122
  31.3 4.7 %collective-permute-start.2 = (f32[64,1,128]{2,1,0:T(1,128)S(1)}, f32[64,1,128]{2,1,0:T(1,128)S(1)}, u32[]{:S(2)}, u32[]{:S(2)}) collective-permute-start(f32[64,1,128]{2,1,0:T(1,128)S(1)} %get-tuple-element.99), channel_id=1, source_target_pairs={{0,4},{4,8},{8,12},{12,16},{16,20},{20,24},{24,28},{1,5},{5,9},{9,... | collective-permute-start | bytes 98312 | tf_op jit(solution)/shard_map/ppermute | solution.py:25
  34.7 4.7 %collective-permute-start.3 = (f32[64,1,128]{2,1,0:T(1,128)S(1)}, f32[64,1,128]{2,1,0:T(1,128)S(1)}, u32[]{:S(2)}, u32[]{:S(2)}) collective-permute-start(f32[64,1,128]{2,1,0:T(1,128)S(1)} %get-tuple-element.100), channel_id=1, source_target_pairs={{4,0},{8,4},{12,8},{16,12},{20,16},{24,20},{28,24},{5,1},{9,5},{13... | collective-permute-start | bytes 98312 | tf_op jit(solution)/shard_map/ppermute | solution.py:27
  39.3 17.9 %copy-start.4 = (f32[64,1,128]{2,1,0:T(1,128)}, f32[64,1,128]{2,1,0:T(1,128)S(1)}, u32[]{:S(2)}) copy-start(f32[64,1,128]{2,1,0:T(1,128)S(1)} %collective-permute-done.3) | copy-start | bytes 98308
  39.4 9.2 %copy-start.3 = (f32[39,2048]{1,0:T(8,128)S(1)}, f32[39,2048]{1,0:T(8,128)}, u32[]{:S(2)}) copy-start(f32[39,2048]{1,0:T(8,128)} %param.13) | copy-start | bytes 958468
  40.5 12.6 %collective-permute-start.4 = (f32[64,10,1]{2,1,0:T(8,128)}, f32[64,10,1]{2,1,0:T(8,128)S(1)}, u32[]{:S(2)}, u32[]{:S(2)}) collective-permute-start(f32[64,10,1]{2,1,0:T(8,128)} %get-tuple-element.90), channel_id=1, source_target_pairs={{0,1},{1,2},{2,3},{4,5},{5,6},{6,7},{8,9},{9,10},{10,11},{12,13},{... | collective-permute-start | bytes 7688 | tf_op jit(solution)/shard_map/ppermute | solution.py:25
  46.7 10.5 %collective-permute-start.5 = (f32[64,10,1]{2,1,0:T(8,128)S(1)}, f32[64,10,1]{2,1,0:T(8,128)S(1)}, u32[]{:S(2)}, u32[]{:S(2)}) collective-permute-start(f32[64,10,1]{2,1,0:T(8,128)S(1)} %get-tuple-element.89), channel_id=1, source_target_pairs={{1,0},{2,1},{3,2},{5,4},{6,5},{7,6},{9,8},{10,9},{11,10},{13,12},{... | collective-permute-start | bytes 7688 | tf_op jit(solution)/shard_map/ppermute | solution.py:27
  59.3 6.4 %collective-permute-start.6 = (f32[64,1,128]{2,1,0:T(1,128)S(1)}, f32[64,1,128]{2,1,0:T(1,128)S(1)}, u32[]{:S(2)}, u32[]{:S(2)}) collective-permute-start(f32[64,1,128]{2,1,0:T(1,128)S(1)} %get-tuple-element.97), channel_id=1, source_target_pairs={{0,4},{4,8},{8,12},{12,16},{16,20},{20,24},{24,28},{1,5},{5,9},{9,... | collective-permute-start | bytes 98312 | tf_op jit(solution)/shard_map/ppermute | solution.py:25
  63.3 4.7 %collective-permute-start.7 = (f32[64,1,128]{2,1,0:T(1,128)S(1)}, f32[64,1,128]{2,1,0:T(1,128)S(1)}, u32[]{:S(2)}, u32[]{:S(2)}) collective-permute-start(f32[64,1,128]{2,1,0:T(1,128)S(1)} %get-tuple-element.98), channel_id=1, source_target_pairs={{4,0},{8,4},{12,8},{16,12},{20,16},{24,20},{28,24},{5,1},{9,5},{13... | collective-permute-start | bytes 98312 | tf_op jit(solution)/shard_map/ppermute | solution.py:27
  68.1 11.2 %all-to-all-start = ((f32[8,1,1248]{2,1,0:T(1,128)}), f32[8,1,1248]{2,1,0:T(1,128)S(1)}, u32[]{:S(2)}, u32[]{:S(2)}) async-start(f32[8,1,1248]{2,1,0:T(1,128)} %reshape.58), calls=%async_computation | async-start | bytes 81920 | tf_op jit(solution)/shard_map/all_to_all | solution.py:121
  72.6 9.6 %collective-permute-start.8 = (f32[64,10,1]{2,1,0:T(8,128)S(1)}, f32[64,10,1]{2,1,0:T(8,128)S(1)}, u32[]{:S(2)}, u32[]{:S(2)}) collective-permute-start(f32[64,10,1]{2,1,0:T(8,128)S(1)} %get-tuple-element.88), channel_id=1, source_target_pairs={{0,1},{1,2},{2,3},{4,5},{5,6},{6,7},{8,9},{9,10},{10,11},{12,13},{... | collective-permute-start | bytes 7688 | tf_op jit(solution)/shard_map/ppermute | solution.py:25
  76.1 10.5 %collective-permute-start.9 = (f32[64,10,1]{2,1,0:T(8,128)S(1)}, f32[64,10,1]{2,1,0:T(8,128)S(1)}, u32[]{:S(2)}, u32[]{:S(2)}) collective-permute-start(f32[64,10,1]{2,1,0:T(8,128)S(1)} %get-tuple-element.87), channel_id=1, source_target_pairs={{1,0},{2,1},{3,2},{5,4},{6,5},{7,6},{9,8},{10,9},{11,10},{13,12},{... | collective-permute-start | bytes 7688 | tf_op jit(solution)/shard_map/ppermute | solution.py:27
  88.0 5.3 %collective-permute-start.10 = (f32[64,1,128]{2,1,0:T(1,128)S(1)}, f32[64,1,128]{2,1,0:T(1,128)S(1)}, u32[]{:S(2)}, u32[]{:S(2)}) collective-permute-start(f32[64,1,128]{2,1,0:T(1,128)S(1)} %get-tuple-element.95), channel_id=1, source_target_pairs={{0,4},{4,8},{8,12},{12,16},{16,20},{20,24},{24,28},{1,5},{5,9},{9,... | collective-permute-start | bytes 98312 | tf_op jit(solution)/shard_map/ppermute | solution.py:25
  91.7 4.7 %collective-permute-start.11 = (f32[64,1,128]{2,1,0:T(1,128)S(1)}, f32[64,1,128]{2,1,0:T(1,128)S(1)}, u32[]{:S(2)}, u32[]{:S(2)}) collective-permute-start(f32[64,1,128]{2,1,0:T(1,128)S(1)} %get-tuple-element.96), channel_id=1, source_target_pairs={{4,0},{8,4},{12,8},{16,12},{20,16},{24,20},{28,24},{5,1},{9,5},{13... | collective-permute-start | bytes 98312 | tf_op jit(solution)/shard_map/ppermute | solution.py:27
  96.7 9.2 %collective-permute-start.12 = (f32[64,10,1]{2,1,0:T(8,128)S(1)}, f32[64,10,1]{2,1,0:T(8,128)S(1)}, u32[]{:S(2)}, u32[]{:S(2)}) collective-permute-start(f32[64,10,1]{2,1,0:T(8,128)S(1)} %get-tuple-element.86), channel_id=1, source_target_pairs={{0,1},{1,2},{2,3},{4,5},{5,6},{6,7},{8,9},{9,10},{10,11},{12,13},{... | collective-permute-start | bytes 7688 | tf_op jit(solution)/shard_map/ppermute | solution.py:25
  99.8 10.5 %collective-permute-start.13 = (f32[64,10,1]{2,1,0:T(8,128)S(1)}, f32[64,10,1]{2,1,0:T(8,128)S(1)}, u32[]{:S(2)}, u32[]{:S(2)}) collective-permute-start(f32[64,10,1]{2,1,0:T(8,128)S(1)} %get-tuple-element.85), channel_id=1, source_target_pairs={{1,0},{2,1},{3,2},{5,4},{6,5},{7,6},{9,8},{10,9},{11,10},{13,12},{... | collective-permute-start | bytes 7688 | tf_op jit(solution)/shard_map/ppermute | solution.py:27
  111.6 5.6 %collective-permute-start.14 = (f32[64,1,128]{2,1,0:T(1,128)S(1)}, f32[64,1,128]{2,1,0:T(1,128)S(1)}, u32[]{:S(2)}, u32[]{:S(2)}) collective-permute-start(f32[64,1,128]{2,1,0:T(1,128)S(1)} %get-tuple-element.93), channel_id=1, source_target_pairs={{0,4},{4,8},{8,12},{12,16},{16,20},{20,24},{24,28},{1,5},{5,9},{9,... | collective-permute-start | bytes 98312 | tf_op jit(solution)/shard_map/ppermute | solution.py:25
  115.7 4.7 %collective-permute-start.15 = (f32[64,1,128]{2,1,0:T(1,128)S(1)}, f32[64,1,128]{2,1,0:T(1,128)S(1)}, u32[]{:S(2)}, u32[]{:S(2)}) collective-permute-start(f32[64,1,128]{2,1,0:T(1,128)S(1)} %get-tuple-element.94), channel_id=1, source_target_pairs={{4,0},{8,4},{12,8},{16,12},{20,16},{24,20},{28,24},{5,1},{9,5},{13... | collective-permute-start | bytes 98312 | tf_op jit(solution)/shard_map/ppermute | solution.py:27
  120.6 9.2 %collective-permute-start.16 = (f32[64,10,1]{2,1,0:T(8,128)S(1)}, f32[64,10,1]{2,1,0:T(8,128)S(1)}, u32[]{:S(2)}, u32[]{:S(2)}) collective-permute-start(f32[64,10,1]{2,1,0:T(8,128)S(1)} %get-tuple-element.84), channel_id=1, source_target_pairs={{0,1},{1,2},{2,3},{4,5},{5,6},{6,7},{8,9},{9,10},{10,11},{12,13},{... | collective-permute-start | bytes 7688 | tf_op jit(solution)/shard_map/ppermute | solution.py:25
  123.7 10.5 %collective-permute-start.17 = (f32[64,10,1]{2,1,0:T(8,128)S(1)}, f32[64,10,1]{2,1,0:T(8,128)S(1)}, u32[]{:S(2)}, u32[]{:S(2)}) collective-permute-start(f32[64,10,1]{2,1,0:T(8,128)S(1)} %get-tuple-element.83), channel_id=1, source_target_pairs={{1,0},{2,1},{3,2},{5,4},{6,5},{7,6},{9,8},{10,9},{11,10},{13,12},{... | collective-permute-start | bytes 7688 | tf_op jit(solution)/shard_map/ppermute | solution.py:27
  (8 other events, 17.3 us)
where the time goes:
time: 137 us; the launch traced here: 136 us
  starting transfers between devices  59.8 us (44%)
  waiting for transfers between devices  41.1 us (30%)
  matrix products  11.8 us (9%)
  other arithmetic  9.87 us (7%)
  local copies, waits for them, and re-layouts  8.97 us (7%)
  loops' own time  2.72 us (2%)
  between operations  1.92 us (1%)
    ppermute x8, starting transfers between devices, with_halo(): lax.ppermute(tail, axis, [(i, (i + 1) % count) for i in range(ends)])  31 us
    ppermute x8, waiting for transfers between devices, with_halo(): lax.ppermute(head, axis, [((i + 1) % count, i) for i in range(ends)])  29 us
    ppermute x8, starting transfers between devices, with_halo(): lax.ppermute(head, axis, [((i + 1) % count, i) for i in range(ends)])  12.9 us
    ppermute x8, waiting for transfers between devices, with_halo(): lax.ppermute(tail, axis, [(i, (i + 1) % count) for i in range(ends)])  12.1 us
    all_to_all x1, starting transfers between devices, shards(): lax.all_to_all(occupied, 'gx', split_axis=1, concat_axis=1, tiled=True)  6.4 us
    dot_general x4, matrix products, one_block(): lax.dot_general(left_table, right_table, (((0,), (0,)), ((), ())), prefer...  6.01 us
    ppermute x2, starting transfers between devices, shifted(): return lax.ppermute(block, axis, route)  5.28 us
    dot_general x8, matrix products, network_rates(): jnp.dot(coupling, occupancy, precision=lax.Precision.HIGHEST, preferred_e...  5.17 us
  transfers between devices with their start and end apart: 20, of which 12 were waited for; matrix products, arithmetic and copies ran while one was open for 8% of the time, Pallas kernels for 0%

commit v1 on v0

--- a/solution.py
+++ b/solution.py
@@ -118,7 +118,10 @@
     )
     occupied = jnp.sum(placing, axis=0)[None, :]
     received, arrived = (
-        lax.all_to_all(outgoing, "gx", split_axis=1, concat_axis=1, tiled=True),
+        jnp.concatenate(
+            lax.all_to_all(jnp.stack(jnp.split(outgoing, lax.axis_size("gx"), axis=1)), "gx", 0, 0),
+            axis=1,
+        ),
         lax.all_to_all(occupied, "gx", split_axis=1, concat_axis=1, tiled=True),
     )
     new_state = advance(cell_state, coupling, basal_rate, half_sat, decay_rate)

time: 137 us -> 137 us (level)
  transfers between devices with their start and end apart: 20 -> 20, of which waited for: 12 -> 12; matrix products, arithmetic and copies ran while one was open for 8% -> 7% of each run, Pallas kernels for 0% -> 0%
where the time goes in v1:
time: 137 us; the launch traced here: 136 us
  starting transfers between devices  59.9 us (44%)
  waiting for transfers between devices  42.2 us (31%)
  matrix products  11.8 us (9%)
  other arithmetic  9.07 us (7%)
  local copies, waits for them, and re-layouts  8.7 us (6%)
  loops' own time  2.72 us (2%)
  between operations  1.91 us (1%)
    ppermute x8, starting transfers between devices, with_halo(): lax.ppermute(tail, axis, [(i, (i + 1) % count) for i in range(ends)])  31.2 us
    ppermute x8, waiting for transfers between devices, with_halo(): lax.ppermute(head, axis, [((i + 1) % count, i) for i in range(ends)])  29.4 us
    ppermute x8, starting transfers between devices, with_halo(): lax.ppermute(head, axis, [((i + 1) % count, i) for i in range(ends)])  12.9 us
    ppermute x8, waiting for transfers between devices, with_halo(): lax.ppermute(tail, axis, [(i, (i + 1) % count) for i in range(ends)])  12.7 us
    all_to_all x1, starting transfers between devices, shards(): lax.all_to_all(occupied, 'gx', split_axis=1, concat_axis=1, tiled=True)  6.39 us
    dot_general x4, matrix products, one_block(): lax.dot_general(left_table, right_table, (((0,), (0,)), ((), ())), prefer...  6.01 us
    ppermute x2, starting transfers between devices, shifted(): return lax.ppermute(block, axis, route)  5.28 us
    dot_general x8, matrix products, network_rates(): jnp.dot(coupling, occupancy, precision=lax.Precision.HIGHEST, preferred_e...  5.17 us
  transfers between devices with their start and end apart: 20, of which 12 were waited for; matrix products, arithmetic and copies ran while one was open for 7% of the time, Pallas kernels for 0%

profile of v1, /device:TPU:1, one launch (start us, length us, event | category | flops | bytes accessed | tf_op | source)
XLA Modules:
  0.0 136.2 jit_solution(12604600258027304712)
XLA Ops:
  6.1 12.0 %while.11 = (s32[]{:T(128)}, f32[1536,128]{1,0:T(8,128)S(1)}, s32[4]{0:T(128)S(1)}, s32[2048]{0:T(1024)S(1)}, s32[2048]{0:T(1024)S(1)}, /*index=5*/bf16[2048]{0:...) while((s32[]{:T(128)}, f32[1536,128]{1,0:T(8,128)S(1)}, s32[4]{0:T(128)S(1)}, ...), condition=%wide.region_4.5_spmd.clone, body=%wide.region_3.4_spmd.clone.sunk | while | flops 202637312 | bytes 1588405 | solution.py:74
  18.2 4.0 %collective-permute-start = (bf16[64,8,128]{2,1,0:T(8,128)(2,1)S(1)}, bf16[64,8,128]{2,1,0:T(8,128)(2,1)S(1)}, u32[]{:S(2)}, u32[]{:S(2)}) collective-permute-start(bf16[64,8,128]{2,1,0:T(8,128)(2,1)S(1)} %get-tuple-element.91), channel_id=1, source_target_pairs={{0,4},{4,8},{8,12},{12,16},{16,20},{20,24},{24,28},{1,5},{5,9},{9,... | collective-permute-start | bytes 393224 | tf_op jit(solution)/shard_map/ppermute | solution.py:14
  24.7 6.4 %all-to-all-start.1 = ((f32[1,8,32]{2,0,1:T(1,128)}), f32[1,8,32]{2,0,1:T(1,128)S(1)}, u32[]{:S(2)}, u32[]{:S(2)}) async-start(f32[1,8,32]{2,0,1:T(1,128)} %all_to_all.10), calls=%async_computation.1 | async-start | bytes 8192 | tf_op jit(solution)/shard_map/all_to_all | solution.py:125
  32.9 3.4 %collective-permute-start.2 = (f32[64,1,128]{2,1,0:T(1,128)S(1)}, f32[64,1,128]{2,1,0:T(1,128)S(1)}, u32[]{:S(2)}, u32[]{:S(2)}) collective-permute-start(f32[64,1,128]{2,1,0:T(1,128)S(1)} %get-tuple-element.99), channel_id=1, source_target_pairs={{0,4},{4,8},{8,12},{12,16},{16,20},{20,24},{24,28},{1,5},{5,9},{9,... | collective-permute-start | bytes 98312 | tf_op jit(solution)/shard_map/ppermute | solution.py:25
  37.6 3.3 %collective-permute-done.3 = f32[64,1,128]{2,1,0:T(1,128)S(1)} collective-permute-done((f32[64,1,128]{2,1,0:T(1,128)S(1)}, f32[64,1,128]{2,1,0:T(1,128)S(1)}, u32[]{:S(2)}, u32[]{:S(2)}) %collective-permute-start.3) | collective-permute-done | bytes 32800 | tf_op jit(solution)/shard_map/ppermute | solution.py:27
  41.2 6.2 %collective-permute-start.4 = (f32[64,10,1]{2,1,0:T(8,128)S(1)}, f32[64,10,1]{2,1,0:T(8,128)S(1)}, u32[]{:S(2)}, u32[]{:S(2)}) collective-permute-start(f32[64,10,1]{2,1,0:T(8,128)S(1)} %get-tuple-element.90), channel_id=1, source_target_pairs={{0,1},{1,2},{2,3},{4,5},{5,6},{6,7},{8,9},{9,10},{10,11},{12,13},{... | collective-permute-start | bytes 7688 | tf_op jit(solution)/shard_map/ppermute | solution.py:25
  49.4 4.1 %collective-permute-done.4 = f32[64,10,1]{2,1,0:T(8,128)S(1)} collective-permute-done((f32[64,10,1]{2,1,0:T(8,128)S(1)}, f32[64,10,1]{2,1,0:T(8,128)S(1)}, u32[]{:S(2)}, u32[]{:S(2)}) %collective-permute-start.4) | collective-permute-done | bytes 2592 | tf_op jit(solution)/shard_map/ppermute | solution.py:25
  53.6 4.4 %collective-permute-done.5 = f32[64,10,1]{2,1,0:T(8,128)S(1)} collective-permute-done((f32[64,10,1]{2,1,0:T(8,128)S(1)}, f32[64,10,1]{2,1,0:T(8,128)S(1)}, u32[]{:S(2)}, u32[]{:S(2)}) %collective-permute-start.5) | collective-permute-done | bytes 2592 | tf_op jit(solution)/shard_map/ppermute | solution.py:27
  59.3 4.1 %collective-permute-start.6 = (f32[64,1,128]{2,1,0:T(1,128)S(1)}, f32[64,1,128]{2,1,0:T(1,128)S(1)}, u32[]{:S(2)}, u32[]{:S(2)}) collective-permute-start(f32[64,1,128]{2,1,0:T(1,128)S(1)} %get-tuple-element.97), channel_id=1, source_target_pairs={{0,4},{4,8},{8,12},{12,16},{16,20},{20,24},{24,28},{1,5},{5,9},{9,... | collective-permute-start | bytes 98312 | tf_op jit(solution)/shard_map/ppermute | solution.py:25
  65.7 2.4 %collective-permute-done.7 = f32[64,1,128]{2,1,0:T(1,128)S(1)} collective-permute-done((f32[64,1,128]{2,1,0:T(1,128)S(1)}, f32[64,1,128]{2,1,0:T(1,128)S(1)}, u32[]{:S(2)}, u32[]{:S(2)}) %collective-permute-start.7) | collective-permute-done | bytes 32800 | tf_op jit(solution)/shard_map/ppermute | solution.py:27
  68.1 4.2 %all-to-all-start = ((f32[8,1,1248]{2,1,0:T(1,128)}), f32[8,1,1248]{2,1,0:T(1,128)S(1)}, u32[]{:S(2)}, u32[]{:S(2)}) async-start(f32[8,1,1248]{2,1,0:T(1,128)} %reshape.64), calls=%async_computation | async-start | bytes 81920 | tf_op jit(solution)/shard_map/all_to_all | solution.py:122
  72.5 3.5 %collective-permute-start.8 = (f32[64,10,1]{2,1,0:T(8,128)S(1)}, f32[64,10,1]{2,1,0:T(8,128)S(1)}, u32[]{:S(2)}, u32[]{:S(2)}) collective-permute-start(f32[64,10,1]{2,1,0:T(8,128)S(1)} %get-tuple-element.88), channel_id=1, source_target_pairs={{0,1},{1,2},{2,3},{4,5},{5,6},{6,7},{8,9},{9,10},{10,11},{12,13},{... | collective-permute-start | bytes 7688 | tf_op jit(solution)/shard_map/ppermute | solution.py:25
  82.1 4.4 %collective-permute-done.9 = f32[64,10,1]{2,1,0:T(8,128)S(1)} collective-permute-done((f32[64,10,1]{2,1,0:T(8,128)S(1)}, f32[64,10,1]{2,1,0:T(8,128)S(1)}, u32[]{:S(2)}, u32[]{:S(2)}) %collective-permute-start.9) | collective-permute-done | bytes 2592 | tf_op jit(solution)/shard_map/ppermute | solution.py:27
  87.9 3.7 %collective-permute-start.10 = (f32[64,1,128]{2,1,0:T(1,128)S(1)}, f32[64,1,128]{2,1,0:T(1,128)S(1)}, u32[]{:S(2)}, u32[]{:S(2)}) collective-permute-start(f32[64,1,128]{2,1,0:T(1,128)S(1)} %get-tuple-element.95), channel_id=1, source_target_pairs={{0,4},{4,8},{8,12},{12,16},{16,20},{20,24},{24,28},{1,5},{5,9},{9,... | collective-permute-start | bytes 98312 | tf_op jit(solution)/shard_map/ppermute | solution.py:25
  93.2 3.1 %collective-permute-done.11 = f32[64,1,128]{2,1,0:T(1,128)S(1)} collective-permute-done((f32[64,1,128]{2,1,0:T(1,128)S(1)}, f32[64,1,128]{2,1,0:T(1,128)S(1)}, u32[]{:S(2)}, u32[]{:S(2)}) %collective-permute-start.11) | collective-permute-done | bytes 32800 | tf_op jit(solution)/shard_map/ppermute | solution.py:27
  96.6 3.1 %collective-permute-start.12 = (f32[64,10,1]{2,1,0:T(8,128)S(1)}, f32[64,10,1]{2,1,0:T(8,128)S(1)}, u32[]{:S(2)}, u32[]{:S(2)}) collective-permute-start(f32[64,10,1]{2,1,0:T(8,128)S(1)} %get-tuple-element.86), channel_id=1, source_target_pairs={{0,1},{1,2},{2,3},{4,5},{5,6},{6,7},{8,9},{9,10},{10,11},{12,13},{... | collective-permute-start | bytes 7688 | tf_op jit(solution)/shard_map/ppermute | solution.py:25
  99.7 1.9 %collective-permute-start.13 = (f32[64,10,1]{2,1,0:T(8,128)S(1)}, f32[64,10,1]{2,1,0:T(8,128)S(1)}, u32[]{:S(2)}, u32[]{:S(2)}) collective-permute-start(f32[64,10,1]{2,1,0:T(8,128)S(1)} %get-tuple-element.85), channel_id=1, source_target_pairs={{1,0},{2,1},{3,2},{5,4},{6,5},{7,6},{9,8},{10,9},{11,10},{13,12},{... | collective-permute-start | bytes 7688 | tf_op jit(solution)/shard_map/ppermute | solution.py:27
  101.9 3.9 %collective-permute-done.12 = f32[64,10,1]{2,1,0:T(8,128)S(1)} collective-permute-done((f32[64,10,1]{2,1,0:T(8,128)S(1)}, f32[64,10,1]{2,1,0:T(8,128)S(1)}, u32[]{:S(2)}, u32[]{:S(2)}) %collective-permute-start.12) | collective-permute-done | bytes 2592 | tf_op jit(solution)/shard_map/ppermute | solution.py:25
  105.8 4.4 %collective-permute-done.13 = f32[64,10,1]{2,1,0:T(8,128)S(1)} collective-permute-done((f32[64,10,1]{2,1,0:T(8,128)S(1)}, f32[64,10,1]{2,1,0:T(8,128)S(1)}, u32[]{:S(2)}, u32[]{:S(2)}) %collective-permute-start.13) | collective-permute-done | bytes 2592 | tf_op jit(solution)/shard_map/ppermute | solution.py:27
  111.6 4.1 %collective-permute-start.14 = (f32[64,1,128]{2,1,0:T(1,128)S(1)}, f32[64,1,128]{2,1,0:T(1,128)S(1)}, u32[]{:S(2)}, u32[]{:S(2)}) collective-permute-start(f32[64,1,128]{2,1,0:T(1,128)S(1)} %get-tuple-element.93), channel_id=1, source_target_pairs={{0,4},{4,8},{8,12},{12,16},{16,20},{20,24},{24,28},{1,5},{5,9},{9,... | collective-permute-start | bytes 98312 | tf_op jit(solution)/shard_map/ppermute | solution.py:25
  117.2 3.1 %collective-permute-done.15 = f32[64,1,128]{2,1,0:T(1,128)S(1)} collective-permute-done((f32[64,1,128]{2,1,0:T(1,128)S(1)}, f32[64,1,128]{2,1,0:T(1,128)S(1)}, u32[]{:S(2)}, u32[]{:S(2)}) %collective-permute-start.15) | collective-permute-done | bytes 32800 | tf_op jit(solution)/shard_map/ppermute | solution.py:27
  120.6 3.1 %collective-permute-start.16 = (f32[64,10,1]{2,1,0:T(8,128)S(1)}, f32[64,10,1]{2,1,0:T(8,128)S(1)}, u32[]{:S(2)}, u32[]{:S(2)}) collective-permute-start(f32[64,10,1]{2,1,0:T(8,128)S(1)} %get-tuple-element.84), channel_id=1, source_target_pairs={{0,1},{1,2},{2,3},{4,5},{5,6},{6,7},{8,9},{9,10},{10,11},{12,13},{... | collective-permute-start | bytes 7688 | tf_op jit(solution)/shard_map/ppermute | solution.py:25
  126.5 3.3 %collective-permute-done.16 = f32[64,10,1]{2,1,0:T(8,128)S(1)} collective-permute-done((f32[64,10,1]{2,1,0:T(8,128)S(1)}, f32[64,10,1]{2,1,0:T(8,128)S(1)}, u32[]{:S(2)}, u32[]{:S(2)}) %collective-permute-start.16) | collective-permute-done | bytes 2592 | tf_op jit(solution)/shard_map/ppermute | solution.py:25
  129.8 4.4 %collective-permute-done.17 = f32[64,10,1]{2,1,0:T(8,128)S(1)} collective-permute-done((f32[64,10,1]{2,1,0:T(8,128)S(1)}, f32[64,10,1]{2,1,0:T(8,128)S(1)}, u32[]{:S(2)}, u32[]{:S(2)}) %collective-permute-start.17) | collective-permute-done | bytes 2592 | tf_op jit(solution)/shard_map/ppermute | solution.py:27
  (123 shorter events, 43.2 us)
Async XLA Ops:
  0.6 2.5 %copy-start.2 = (f32[39,2048]{1,0:T(8,128)S(1)}, f32[39,2048]{1,0:T(8,128)}, u32[]{:S(2)}) copy-start(f32[39,2048]{1,0:T(8,128)} %param.13) | copy-start | bytes 958468
  18.1 5.4 %copy-start.5 = (s32[128,1]{0,1:T(1,128)S(1)}, s32[128,1]{0,1:T(1,128)}, u32[]{:S(2)}) copy-start(s32[128,1]{0,1:T(1,128)} %param.21) | copy-start | bytes 1540
  18.1 13.4 %copy-start.7 = (s32[128]{0:T(128)S(1)}, s32[128]{0:T(128)}, u32[]{:S(2)}) copy-start(s32[128]{0:T(128)} %param.20) | copy-start | bytes 1540
  18.2 14.6 %collective-permute-start = (bf16[64,8,128]{2,1,0:T(8,128)(2,1)S(1)}, bf16[64,8,128]{2,1,0:T(8,128)(2,1)S(1)}, u32[]{:S(2)}, u32[]{:S(2)}) collective-permute-start(bf16[64,8,128]{2,1,0:T(8,128)(2,1)S(1)} %get-tuple-element.91), channel_id=1, source_target_pairs={{0,4},{4,8},{8,12},{12,16},{16,20},{20,24},{24,28},{1,5},{5,9},{9,... | collective-permute-start | bytes 393224 | tf_op jit(solution)/shard_map/ppermute | solution.py:14
  22.2 10.6 %collective-permute-start.1 = (bf16[64,8,128]{2,1,0:T(8,128)(2,1)S(1)}, bf16[64,8,128]{2,1,0:T(8,128)(2,1)S(1)}, u32[]{:S(2)}, u32[]{:S(2)}) collective-permute-start(bf16[64,8,128]{2,1,0:T(8,128)(2,1)S(1)} %get-tuple-element.92), channel_id=1, source_target_pairs={{4,0},{8,4},{12,8},{16,12},{20,16},{24,20},{28,24},{5,1},{9,5},{13... | collective-permute-start | bytes 393224 | tf_op jit(solution)/shard_map/ppermute | solution.py:14
  23.5 9.3 %copy-start.3 = (f32[64,8,128]{2,1,0:T(8,128)S(1)}, f32[64,8,128]{2,1,0:T(8,128)}, u32[]{:S(2)}) copy-start(f32[64,8,128]{2,1,0:T(8,128)} %param.23) | copy-start | bytes 786436
  24.7 43.4 %all-to-all-start.1 = ((f32[1,8,32]{2,0,1:T(1,128)}), f32[1,8,32]{2,0,1:T(1,128)S(1)}, u32[]{:S(2)}, u32[]{:S(2)}) async-start(f32[1,8,32]{2,0,1:T(1,128)} %all_to_all.10), calls=%async_computation.1 | async-start | bytes 8192 | tf_op jit(solution)/shard_map/all_to_all | solution.py:125
  32.9 4.8 %collective-permute-start.2 = (f32[64,1,128]{2,1,0:T(1,128)S(1)}, f32[64,1,128]{2,1,0:T(1,128)S(1)}, u32[]{:S(2)}, u32[]{:S(2)}) collective-permute-start(f32[64,1,128]{2,1,0:T(1,128)S(1)} %get-tuple-element.99), channel_id=1, source_target_pairs={{0,4},{4,8},{8,12},{12,16},{16,20},{20,24},{24,28},{1,5},{5,9},{9,... | collective-permute-start | bytes 98312 | tf_op jit(solution)/shard_map/ppermute | solution.py:25
  36.2 4.7 %collective-permute-start.3 = (f32[64,1,128]{2,1,0:T(1,128)S(1)}, f32[64,1,128]{2,1,0:T(1,128)S(1)}, u32[]{:S(2)}, u32[]{:S(2)}) collective-permute-start(f32[64,1,128]{2,1,0:T(1,128)S(1)} %get-tuple-element.100), channel_id=1, source_target_pairs={{4,0},{8,4},{12,8},{16,12},{20,16},{24,20},{28,24},{5,1},{9,5},{13... | collective-permute-start | bytes 98312 | tf_op jit(solution)/shard_map/ppermute | solution.py:27
  41.2 12.3 %collective-permute-start.4 = (f32[64,10,1]{2,1,0:T(8,128)S(1)}, f32[64,10,1]{2,1,0:T(8,128)S(1)}, u32[]{:S(2)}, u32[]{:S(2)}) collective-permute-start(f32[64,10,1]{2,1,0:T(8,128)S(1)} %get-tuple-element.90), channel_id=1, source_target_pairs={{0,1},{1,2},{2,3},{4,5},{5,6},{6,7},{8,9},{9,10},{10,11},{12,13},{... | collective-permute-start | bytes 7688 | tf_op jit(solution)/shard_map/ppermute | solution.py:25
  47.4 10.5 %collective-permute-start.5 = (f32[64,10,1]{2,1,0:T(8,128)S(1)}, f32[64,10,1]{2,1,0:T(8,128)S(1)}, u32[]{:S(2)}, u32[]{:S(2)}) collective-permute-start(f32[64,10,1]{2,1,0:T(8,128)S(1)} %get-tuple-element.89), channel_id=1, source_target_pairs={{1,0},{2,1},{3,2},{5,4},{6,5},{7,6},{9,8},{10,9},{11,10},{13,12},{... | collective-permute-start | bytes 7688 | tf_op jit(solution)/shard_map/ppermute | solution.py:27
  59.3 6.4 %collective-permute-start.6 = (f32[64,1,128]{2,1,0:T(1,128)S(1)}, f32[64,1,128]{2,1,0:T(1,128)S(1)}, u32[]{:S(2)}, u32[]{:S(2)}) collective-permute-start(f32[64,1,128]{2,1,0:T(1,128)S(1)} %get-tuple-element.97), channel_id=1, source_target_pairs={{0,4},{4,8},{8,12},{12,16},{16,20},{20,24},{24,28},{1,5},{5,9},{9,... | collective-permute-start | bytes 98312 | tf_op jit(solution)/shard_map/ppermute | solution.py:25
  63.4 4.7 %collective-permute-start.7 = (f32[64,1,128]{2,1,0:T(1,128)S(1)}, f32[64,1,128]{2,1,0:T(1,128)S(1)}, u32[]{:S(2)}, u32[]{:S(2)}) collective-permute-start(f32[64,1,128]{2,1,0:T(1,128)S(1)} %get-tuple-element.98), channel_id=1, source_target_pairs={{4,0},{8,4},{12,8},{16,12},{20,16},{24,20},{28,24},{5,1},{9,5},{13... | collective-permute-start | bytes 98312 | tf_op jit(solution)/shard_map/ppermute | solution.py:27
  68.1 11.1 %all-to-all-start = ((f32[8,1,1248]{2,1,0:T(1,128)}), f32[8,1,1248]{2,1,0:T(1,128)S(1)}, u32[]{:S(2)}, u32[]{:S(2)}) async-start(f32[8,1,1248]{2,1,0:T(1,128)} %reshape.64), calls=%async_computation | async-start | bytes 81920 | tf_op jit(solution)/shard_map/all_to_all | solution.py:122
  72.5 9.6 %collective-permute-start.8 = (f32[64,10,1]{2,1,0:T(8,128)S(1)}, f32[64,10,1]{2,1,0:T(8,128)S(1)}, u32[]{:S(2)}, u32[]{:S(2)}) collective-permute-start(f32[64,10,1]{2,1,0:T(8,128)S(1)} %get-tuple-element.88), channel_id=1, source_target_pairs={{0,1},{1,2},{2,3},{4,5},{5,6},{6,7},{8,9},{9,10},{10,11},{12,13},{... | collective-permute-start | bytes 7688 | tf_op jit(solution)/shard_map/ppermute | solution.py:25
  76.0 10.5 %collective-permute-start.9 = (f32[64,10,1]{2,1,0:T(8,128)S(1)}, f32[64,10,1]{2,1,0:T(8,128)S(1)}, u32[]{:S(2)}, u32[]{:S(2)}) collective-permute-start(f32[64,10,1]{2,1,0:T(8,128)S(1)} %get-tuple-element.87), channel_id=1, source_target_pairs={{1,0},{2,1},{3,2},{5,4},{6,5},{7,6},{9,8},{10,9},{11,10},{13,12},{... | collective-permute-start | bytes 7688 | tf_op jit(solution)/shard_map/ppermute | solution.py:27
  87.9 5.3 %collective-permute-start.10 = (f32[64,1,128]{2,1,0:T(1,128)S(1)}, f32[64,1,128]{2,1,0:T(1,128)S(1)}, u32[]{:S(2)}, u32[]{:S(2)}) collective-permute-start(f32[64,1,128]{2,1,0:T(1,128)S(1)} %get-tuple-element.95), channel_id=1, source_target_pairs={{0,4},{4,8},{8,12},{12,16},{16,20},{20,24},{24,28},{1,5},{5,9},{9,... | collective-permute-start | bytes 98312 | tf_op jit(solution)/shard_map/ppermute | solution.py:25
  91.7 4.7 %collective-permute-start.11 = (f32[64,1,128]{2,1,0:T(1,128)S(1)}, f32[64,1,128]{2,1,0:T(1,128)S(1)}, u32[]{:S(2)}, u32[]{:S(2)}) collective-permute-start(f32[64,1,128]{2,1,0:T(1,128)S(1)} %get-tuple-element.96), channel_id=1, source_target_pairs={{4,0},{8,4},{12,8},{16,12},{20,16},{24,20},{28,24},{5,1},{9,5},{13... | collective-permute-start | bytes 98312 | tf_op jit(solution)/shard_map/ppermute | solution.py:27
  96.6 9.2 %collective-permute-start.12 = (f32[64,10,1]{2,1,0:T(8,128)S(1)}, f32[64,10,1]{2,1,0:T(8,128)S(1)}, u32[]{:S(2)}, u32[]{:S(2)}) collective-permute-start(f32[64,10,1]{2,1,0:T(8,128)S(1)} %get-tuple-element.86), channel_id=1, source_target_pairs={{0,1},{1,2},{2,3},{4,5},{5,6},{6,7},{8,9},{9,10},{10,11},{12,13},{... | collective-permute-start | bytes 7688 | tf_op jit(solution)/shard_map/ppermute | solution.py:25
  99.7 10.5 %collective-permute-start.13 = (f32[64,10,1]{2,1,0:T(8,128)S(1)}, f32[64,10,1]{2,1,0:T(8,128)S(1)}, u32[]{:S(2)}, u32[]{:S(2)}) collective-permute-start(f32[64,10,1]{2,1,0:T(8,128)S(1)} %get-tuple-element.85), channel_id=1, source_target_pairs={{1,0},{2,1},{3,2},{5,4},{6,5},{7,6},{9,8},{10,9},{11,10},{13,12},{... | collective-permute-start | bytes 7688 | tf_op jit(solution)/shard_map/ppermute | solution.py:27
  111.6 5.6 %collective-permute-start.14 = (f32[64,1,128]{2,1,0:T(1,128)S(1)}, f32[64,1,128]{2,1,0:T(1,128)S(1)}, u32[]{:S(2)}, u32[]{:S(2)}) collective-permute-start(f32[64,1,128]{2,1,0:T(1,128)S(1)} %get-tuple-element.93), channel_id=1, source_target_pairs={{0,4},{4,8},{8,12},{12,16},{16,20},{20,24},{24,28},{1,5},{5,9},{9,... | collective-permute-start | bytes 98312 | tf_op jit(solution)/shard_map/ppermute | solution.py:25
  115.6 4.7 %collective-permute-start.15 = (f32[64,1,128]{2,1,0:T(1,128)S(1)}, f32[64,1,128]{2,1,0:T(1,128)S(1)}, u32[]{:S(2)}, u32[]{:S(2)}) collective-permute-start(f32[64,1,128]{2,1,0:T(1,128)S(1)} %get-tuple-element.94), channel_id=1, source_target_pairs={{4,0},{8,4},{12,8},{16,12},{20,16},{24,20},{28,24},{5,1},{9,5},{13... | collective-permute-start | bytes 98312 | tf_op jit(solution)/shard_map/ppermute | solution.py:27
  120.6 9.2 %collective-permute-start.16 = (f32[64,10,1]{2,1,0:T(8,128)S(1)}, f32[64,10,1]{2,1,0:T(8,128)S(1)}, u32[]{:S(2)}, u32[]{:S(2)}) collective-permute-start(f32[64,10,1]{2,1,0:T(8,128)S(1)} %get-tuple-element.84), channel_id=1, source_target_pairs={{0,1},{1,2},{2,3},{4,5},{5,6},{6,7},{8,9},{9,10},{10,11},{12,13},{... | collective-permute-start | bytes 7688 | tf_op jit(solution)/shard_map/ppermute | solution.py:25
  123.7 10.5 %collective-permute-start.17 = (f32[64,10,1]{2,1,0:T(8,128)S(1)}, f32[64,10,1]{2,1,0:T(8,128)S(1)}, u32[]{:S(2)}, u32[]{:S(2)}) collective-permute-start(f32[64,10,1]{2,1,0:T(8,128)S(1)} %get-tuple-element.83), channel_id=1, source_target_pairs={{1,0},{2,1},{3,2},{5,4},{6,5},{7,6},{9,8},{10,9},{11,10},{13,12},{... | collective-permute-start | bytes 7688 | tf_op jit(solution)/shard_map/ppermute | solution.py:27
  (6 other events, 9.4 us)
